TPU v7x, 32 devices: a whole 2x2x4 slice. The times are simulated.
32 devices in a mesh: dp: 4 (over x, core), ctx: 8 (over z, y).
Axes of the slice: x: 2, y: 2, z: 4, core: 2. Of those that a mesh axis runs over, the one named last changes fastest.
Arguments:
- query: bfloat16 [4, 1024, 2048], P('dp', 'ctx'), may hold values from -6 to 6
- keys: bfloat16 [4, 1024, 2048], P('dp', 'ctx'), may hold values from -6 to 6
- values: bfloat16 [4, 1024, 2048], P('dp', 'ctx'), may hold values from -6 to 6
- cotangent: bfloat16 [4, 1024, 2048], P('dp', 'ctx'), may hold values from -6 to 6
- long_filter: bfloat16 [1024, 2048], P('ctx'), may hold values from -1.05 to 1.05, as said below
- short_weights: float32 [3, 3, 2048], replicated, may hold values from -3 to 3
- skip: float32 [2048], replicated, may hold values from -4 to 4
- lengths: int32 [4, 16], P('dp'), may hold values from 1 to 256, 1024 in all within a row
Outputs:
- gated: bfloat16 [4, 1024, 2048], P('dp', 'ctx')
- grad_query: bfloat16 [4, 1024, 2048], P('dp', 'ctx')
- grad_keys: bfloat16 [4, 1024, 2048], P('dp', 'ctx')
- grad_values: bfloat16 [4, 1024, 2048], P('dp', 'ctx')
- grad_filter: float32 [1024, 2048], P('ctx', 'dp')
- grad_short: float32 [3, 3, 2048], replicated
- grad_skip: float32 [2048], replicated
Inputs may be any that keep to these rules, and one draw needn't show every extreme that they name: Each row lists, in order, the lengths of the 16 documents packed into one sequence; they sum to 1024 and the longest is exactly 256. `long_filter`: one filter for every channel over the lags 0 .. 1023.
All inputs are finite; a program needn't handle non-finite values.
Results may differ from a plain program's by a relative error of at most 0.024.
Values may be sent and summed in bfloat16 or wider, within the bound.
No kernel may reach another device: no remote copies, remote signals or barrier semaphores. Data moves between devices by JAX's collectives and lax.ppermute only.
A program may use at most 192 MiB of HBM per device.

v0:
```python
import math
import jax
import jax.numpy as jnp
import ml_dtypes
import numpy as np
from jax import lax
from jax.sharding import PartitionSpec as P


def shifted(x, axis, by):
    length = lax.axis_size(axis)
    pairs = [(i, i + by) for i in range(length) if 0 <= i + by < length]
    return lax.ppermute(x, axis, pairs)


def table_halves(table):
    upper = table.astype(ml_dtypes.bfloat16)
    lower = (table - upper.astype(np.float64)).astype(ml_dtypes.bfloat16)
    return (jnp.asarray(upper), jnp.asarray(lower))


def split_product(form, table, data):
    upper, lower = table_halves(table)
    wide = jnp.float32
    if data.dtype == jnp.bfloat16:
        total = jnp.einsum(form, upper, data, preferred_element_type=wide)
        return total + jnp.einsum(form, lower, data, preferred_element_type=wide)
    data_upper = lax.optimization_barrier(data.astype(jnp.bfloat16))
    data_lower = (data - data_upper.astype(wide)).astype(jnp.bfloat16)
    total = jnp.einsum(form, upper, data_upper, preferred_element_type=wide)
    total = total + jnp.einsum(form, lower, data_upper, preferred_element_type=wide)
    return total + jnp.einsum(form, upper, data_lower, preferred_element_type=wide)


def factors(size):
    bits = size.bit_length() - 1
    inner = 1 << bits // 2
    return (size // inner, inner)


def twiddles(outer, inner, size):
    phase = 2.0 * np.pi * np.outer(np.arange(outer), np.arange(inner)) / size
    cosine = jnp.asarray(np.cos(phase), jnp.float32)[None, :, :, None]
    sine = jnp.asarray(np.sin(phase), jnp.float32)[None, :, :, None]
    return (cosine, sine)


def inner_table(inner, sign):
    phase = 2.0 * np.pi * np.outer(np.arange(inner), np.arange(inner)) / inner
    cosine, sine = (np.cos(phase), sign * np.sin(phase))
    return np.block([[cosine, sine], [-sine, cosine]])


def fft_forward(signal):
    count, length, lanes = signal.shape
    size = 2 * length
    outer, inner = factors(size)
    half = outer // 2
    phase = 2.0 * np.pi * np.outer(np.arange(outer), np.arange(half)) / outer
    first = np.concatenate([np.cos(phase), -np.sin(phase)], 0)
    stage = split_product("kn,snqb->skqb", first, signal.reshape(count, half, inner, lanes))
    real_part, imag_part = (stage[:, :outer], stage[:, outer:])
    cosine, sine = twiddles(outer, inner, size)
    turned = jnp.concatenate(
        [real_part * cosine + imag_part * sine, imag_part * cosine - real_part * sine], 2
    )
    return split_product("ab,skbc->skac", inner_table(inner, 1.0), turned)


def fft_inverse(spectrum, length):
    count, outer, twice, lanes = spectrum.shape
    inner = twice // 2
    size = outer * inner
    half = outer // 2
    stage = split_product("ab,skbc->skac", inner_table(inner, -1.0), spectrum)
    real_part, imag_part = (stage[:, :, :inner], stage[:, :, inner:])
    cosine, sine = twiddles(outer, inner, size)
    turned = jnp.concatenate(
        [real_part * cosine - imag_part * sine, imag_part * cosine + real_part * sine], 1
    )
    phase = 2.0 * np.pi * np.outer(np.arange(half), np.arange(outer)) / outer
    last = np.concatenate([np.cos(phase), -np.sin(phase)], 1) / size
    return split_product("nk,skqb->snqb", last, turned).reshape(count, length, lanes)


def spectral_products(spectra):
    inner = spectra.shape[2] // 2
    parts = [(s[:, :inner], s[:, inner:]) for s in (spectra[0], spectra[1], spectra[2])]
    (f_re, f_im), (m_re, m_im), (g_re, g_im) = parts
    conv = jnp.concatenate([m_re * f_re - m_im * f_im, m_re * f_im + m_im * f_re], 1)
    back = jnp.concatenate([g_re * f_re + g_im * f_im, g_im * f_re - g_re * f_im], 1)
    cross = jnp.concatenate([g_re * m_re + g_im * m_im, g_im * m_re - g_re * m_im], 1)
    return jnp.stack([conv, back, cross])


def local(query, keys, values, cotangent, long_filter, short_weights, skip, lengths):
    parts = lax.axis_size("ctx")
    index = lax.axis_index("ctx")
    groups = lax.axis_size("dp")
    q_rows, k_rows, v_rows, c_rows = (query[0], keys[0], values[0], cotangent[0])
    rows, chans = q_rows.shape
    taps = short_weights.shape[1]
    head = taps - 1
    seq_len = rows * parts
    lanes = chans // parts
    ext = rows + head
    doc_len = lengths[0]
    starts = jnp.cumsum(doc_len) - doc_len
    position = index * rows + jnp.arange(ext, dtype=jnp.int32)
    begin = jnp.max(jnp.where(starts[None, :] <= position[:, None], starts[None, :], 0), axis=1)
    valid = position[None, :] - jnp.arange(taps, dtype=jnp.int32)[:, None] >= begin[None, :]
    valid_after = valid & (position < seq_len)[None, :]
    prev = shifted((q_rows[rows - head :], k_rows[rows - head :], v_rows[rows - head :]), "ctx", 1)
    nxt = shifted((q_rows[:head], k_rows[:head], v_rows[:head], c_rows[:head]), "ctx", -1)
    padded = [
        jnp.concatenate([prev[i], src, nxt[i]], 0).astype(jnp.float32)
        for i, src in enumerate((q_rows, k_rows, v_rows))
    ]

    def short_forward(wide, weights):
        summed = weights[0] * wide[head : head + ext]
        for offset in range(1, taps):
            begin_at = head - offset
            summed = summed + jnp.where(
                valid[offset][:, None], weights[offset] * wide[begin_at : begin_at + ext], 0.0
            )
        return summed.astype(jnp.bfloat16).astype(jnp.float32)

    q_short = short_forward(padded[0], short_weights[0])
    k_short = short_forward(padded[1], short_weights[1])
    v_short = short_forward(padded[2], short_weights[2])
    upstream = jnp.concatenate([c_rows, nxt[3]], 0).astype(jnp.float32)
    mixed = (k_short * v_short).astype(jnp.bfloat16)
    grad_conv = (upstream * q_short).astype(jnp.bfloat16)
    mixed_wide = mixed.astype(jnp.float32)
    grad_wide = grad_conv.astype(jnp.float32)
    sent = jnp.stack([long_filter, mixed[:rows], grad_conv[:rows]])
    columns = lax.all_to_all(sent, "ctx", 2, 1, tiled=True)
    spectra = fft_forward(columns)
    raw = fft_inverse(spectral_products(spectra), seq_len).astype(jnp.bfloat16)
    raw = jnp.concatenate([raw, jnp.zeros((3, head, lanes), raw.dtype)], 1)
    blocks = jnp.stack([raw[:, j * rows : j * rows + ext] for j in range(parts)], 1)
    back = lax.all_to_all(blocks, "ctx", 1, 3, tiled=True).reshape(3, ext, chans)
    back = back.astype(jnp.float32)
    conv = back[0] + skip * mixed_wide
    gated = (q_short[:rows] * conv[:rows]).astype(jnp.bfloat16)
    grad_qs = upstream * conv
    grad_mixed = back[1] + skip * grad_wide
    grad_ks = grad_mixed * v_short
    grad_vs = grad_mixed * k_short

    def short_backward(wide, grad_short, weights):
        grad_source = weights[0] * grad_short[:rows]
        weight_grads = [jnp.sum(wide[head : head + rows] * grad_short[:rows], axis=0)]
        for offset in range(1, taps):
            later = jnp.where(
                valid_after[offset, offset : offset + rows][:, None],
                grad_short[offset : offset + rows],
                0.0,
            )
            grad_source = grad_source + weights[offset] * later
            masked = jnp.where(valid[offset, :rows][:, None], grad_short[:rows], 0.0)
            begin_at = head - offset
            weight_grads.append(jnp.sum(masked * wide[begin_at : begin_at + rows], axis=0))
        return (grad_source, jnp.stack(weight_grads))

    grad_q, short_q = short_backward(padded[0], grad_qs, short_weights[0])
    grad_k, short_k = short_backward(padded[1], grad_ks, short_weights[1])
    grad_v, short_v = short_backward(padded[2], grad_vs, short_weights[2])
    skip_grad = jnp.sum(grad_wide[:rows] * mixed_wide[:rows], axis=0)
    stats = jnp.concatenate(
        [jnp.stack([short_q, short_k, short_v]).reshape(3 * taps, chans), skip_grad[None]], 0
    )
    summed = lax.psum(stats, ("dp", "ctx"))
    filter_part = lax.psum_scatter(back[2, :rows], "dp", scatter_dimension=1, tiled=True)
    scale = 1.0 / (groups * seq_len)
    return (
        gated[None],
        grad_q.astype(jnp.bfloat16)[None],
        grad_k.astype(jnp.bfloat16)[None],
        grad_v.astype(jnp.bfloat16)[None],
        filter_part * scale,
        summed[: 3 * taps].reshape(3, taps, chans) * scale,
        summed[3 * taps] * scale,
    )


def solution(mesh):
    in_specs = (
        P("dp", "ctx", None),
        P("dp", "ctx", None),
        P("dp", "ctx", None),
        P("dp", "ctx", None),
        P("ctx", None),
        P(),
        P(),
        P("dp", None),
    )
    out_specs = (
        P("dp", "ctx", None),
        P("dp", "ctx", None),
        P("dp", "ctx", None),
        P("dp", "ctx", None),
        P("ctx", "dp"),
        P(),
        P(),
    )
    return jax.shard_map(local, mesh=mesh, in_specs=in_specs, out_specs=out_specs, check_vma=False)
```

profile of v0, /device:TPU:0, one launch (start us, length us, event | category | flops | bytes accessed | tf_op | source)
XLA Modules:
  0.0 471.6 jit_solution(2773663166921018954)
XLA Ops:
  8.9 4.9 %collective-permute-start.4 = (bf16[2,2048]{1,0:T(2,128)(2,1)S(1)}, bf16[2,2048]{1,0:T(2,128)(2,1)S(1)}, u32[]{:S(2)}, u32[]{:S(2)}) collective-permute-start(bf16[2,2048]{1,0:T(2,128)(2,1)S(1)} %get-tuple-element.58), channel_id=1, source_target_pairs={{0,1},{1,2},{2,3},{3,4},{4,5},{5,6},{6,7},{8,9},{9,10},{10,11},{11... | collective-permute-start | bytes 24584 | tf_op jit(solution)/shard_map/ppermute | solution.py:13
  15.8 4.5 collective-permute-start.2
  22.5 5.0 %collective-permute-start = (bf16[2,2048]{1,0:T(2,128)(2,1)S(1)}, bf16[2,2048]{1,0:T(2,128)(2,1)S(1)}, u32[]{:S(2)}, u32[]{:S(2)}) collective-permute-start(bf16[2,2048]{1,0:T(2,128)(2,1)S(1)} %get-tuple-element.62), channel_id=1, source_target_pairs={{0,1},{1,2},{2,3},{3,4},{4,5},{5,6},{6,7},{8,9},{9,10},{10,11},{11... | collective-permute-start | bytes 24584 | tf_op jit(solution)/shard_map/ppermute | solution.py:13
  47.6 54.8 %all_to_all.24 = bf16[3,128,2048]{1,0,2:T(4,128)(2,1)S(1)} all-to-all(bf16[3,128,2048]{1,0,2:T(4,128)(2,1)S(1)} %copy.95), channel_id=1, replica_groups=mesh['dp'=4,'ctx'=8] {'ctx'}, dimensions={2} | all-to-all | bytes 3145728 | tf_op jit(solution)/shard_map/all_to_all | solution.py:138
  107.5 5.4 %multiply_add_fusion.1 = (f32[3,64,32,256]{3,1,2,0:T(8,128)}, f32[3,64,32,256]{3,1,2,0:T(8,128)}) fusion(f32[3,128,32,256]{3,1,2,0:T(8,128)S(1)} %add_bitcast_fusion.1, f32[64,32]{0,1:T(8,128)S(1)} %copy-done.44, f32[64,32]{0,1:T(8,128)S(1)} %copy-done.45), kind=kLoop, calls=%fused_computation.20 | loop fusion | flops 9437184 | bytes 25182208 | tf_op jit(solution)/shard_map/add | solution.py:65
  112.9 7.9 %fusion.2 = bf16[3,64,64,256]{3,1,2,0:T(8,128)(2,1)} fusion(f32[3,64,32,256]{3,1,2,0:T(8,128)} %get-tuple-element.39, f32[3,64,32,256]{3,1,2,0:T(8,128)} %get-tuple-element.38), kind=kLoop, calls=%fused_computation.12 | loop fusion | flops 3145728 | bytes 18874368 | tf_op jit(solution)/shard_map/convert_element_type | solution.py:28
  120.8 8.5 %subtract_convert_fusion.2 = bf16[3,64,64,256]{3,1,2,0:T(8,128)(2,1)S(1)} fusion(bf16[3,64,64,256]{3,1,2,0:T(8,128)(2,1)} %fusion.2, f32[3,64,32,256]{3,1,2,0:T(8,128)} %get-tuple-element.39, f32[3,64,32,256]{3,1,2,0:T(8,128)} %get-tuple-element.38), kind=kLoop, calls=%fused_computation.9 | loop fusion | flops 12582912 | bytes 25165824 | tf_op jit(solution)/shard_map/convert_element_type | solution.py:29
  129.3 9.5 %fusion.8 = f32[3,64,256,64]{2,3,1,0:T(8,128)} fusion(bf16[64,64,1,1]{1,0,3,2:T(8,128)(2,1)S(1)} %copy-done.46, bf16[3,64,64,256]{3,1,2,0:T(8,128)(2,1)S(1)} %copy-done.1), kind=kOutput, calls=%fused_computation.22 | convolution fusion | flops 402653184 | bytes 18882560 | tf_op jit(solution)/shard_map/ab,skbc->skac/dot_general | solution.py:30
  138.8 9.5 %fusion.5 = f32[3,64,256,64]{2,3,1,0:T(8,128)} fusion(bf16[64,64,1,1]{1,0,3,2:T(8,128)(2,1)S(1)} %copy-done.46, bf16[3,64,64,256]{3,1,2,0:T(8,128)(2,1)S(1)} %subtract_convert_fusion.2), kind=kOutput, calls=%fused_computation.15 | convolution fusion | flops 402653184 | bytes 18882560 | tf_op jit(solution)/shard_map/ab,skbc->skac/dot_general | solution.py:32
  148.3 14.4 %add_bitcast_fusion = f32[3,64,64,256]{3,2,1,0:T(8,128)} fusion(f32[3,64,256,64]{2,3,1,0:T(8,128)} %fusion.5, f32[3,64,256,64]{2,3,1,0:T(8,128)} %fusion.8, bf16[64,64,1,1]{1,0,3,2:T(8,128)(2,1)S(1)} %copy-done.50, bf16[3,64,64,256]{3,1,2,0:T(8,128)(2,1)S(1)} %copy-done.1), kind=kOutput, calls=%fused_computation.8 | convolution fusion | flops 408944640 | bytes 44048384 | tf_op jit(solution)/shard_map/ab,skbc->skac/dot_general | solution.py:31
  162.8 9.9 %slice_bitcast_fusion.1 = (f32[64,64,256]{2,1,0:T(8,128)S(1)}, f32[64,64,256]{2,1,0:T(8,128)}, f32[64,64,256]{2,1,0:T(8,128)}) fusion(f32[3,64,64,256]{3,2,1,0:T(8,128)} %add_bitcast_fusion), kind=kLoop, calls=%fused_computation.27 | loop fusion | bytes 25165824 | tf_op jit(solution)/shard_map/squeeze | solution.py:88
  172.7 5.5 %multiply_add_fusion.3 = (f32[64,32,256]{2,1,0:T(8,128)}, f32[64,32,256]{2,1,0:T(8,128)}) fusion(f32[64,64,256]{2,1,0:T(8,128)} %get-tuple-element.41, f32[64,64,256]{2,1,0:T(8,128)S(1)} %get-tuple-element.40), kind=kLoop, calls=%fused_computation.37 | loop fusion | flops 3145728 | bytes 12582912 | tf_op jit(solution)/shard_map/add | solution.py:91
  178.2 5.8 %multiply_subtract_fusion.4 = (f32[64,32,256]{2,1,0:T(8,128)}, f32[64,32,256]{2,1,0:T(8,128)}, f32[64,32,256]{2,1,0:T(8,128)S(1)}, f32[64,32,256]{2,1,0:T(8,128)S(1)}) fusion(f32[64,64,256]{2,1,0:T(8,128)S(1)} %get-tuple-element.40, f32[64,64,256]{2,1,0:T(8,128)} %get-tuple-element.42, f32[64,64,256]{2,1,0:T(8,128)S(1)} %copy-done.8), kind=kLoop, calls=%fused_computation.39 | loop fusion | flops 6291456 | bytes 20971520 | tf_op jit(solution)/shard_map/sub | solution.py:90
  184.0 4.8 %maximum_bitcast_fusion.1 = f32[1,64,64,256]{3,2,1,0:T(8,128)} fusion(f32[64,32,256]{2,1,0:T(8,128)} %get-tuple-element.46, f32[64,32,256]{2,1,0:T(8,128)} %get-tuple-element.45), kind=kLoop, calls=%fused_computation.30 | loop fusion | flops 1048576 | bytes 8388608 | tf_op jit(solution)/shard_map/stack | solution.py:93
  193.6 5.4 %fusion.3 = bf16[3,64,64,256]{3,2,1,0:T(8,128)(2,1)S(1)} fusion(f32[1,64,64,256]{3,2,1,0:T(8,128)} %maximum_bitcast_fusion.2, f32[1,64,64,256]{3,2,1,0:T(8,128)} %maximum_bitcast_fusion.1, f32[1,64,64,256]{3,2,1,0:T(8,128)} %maximum_bitcast_fusion), kind=kLoop, calls=%fused_computation.13 | loop fusion | flops 6291456 | bytes 18874368 | tf_op jit(solution)/shard_map/convert_element_type | solution.py:28
  199.0 5.9 %fusion.4 = f32[3,64,256,64]{2,3,1,0:T(8,128)S(1)} fusion(bf16[64,64,1,1]{1,0,3,2:T(8,128)(2,1)S(1)} %copy-done.43, bf16[3,64,64,256]{3,2,1,0:T(8,128)(2,1)S(1)} %fusion.3, f32[1,64,64,256]{3,2,1,0:T(8,128)} %maximum_bitcast_fusion.2, f32[1,64,64,256]{3,2,1,0:T(8,128)} %maximum_bitcast_fusion.1, f32[1,64,64,256]{3,2,1,0:T(8,128)} %maximum_bitcast_fusion), kind=kOutput, calls=%fused_computation.14 | convolution fusion | flops 418381824 | bytes 31465472 | tf_op jit(solution)/shard_map/ab,skbc->skac/dot_general | solution.py:32
  204.9 6.4 %fusion.86 = f32[3,64,256,64]{2,3,1,0:T(8,128)} fusion(bf16[64,64,1,1]{1,0,3,2:T(8,128)(2,1)S(1)} %copy-done.43, bf16[3,64,64,256]{3,2,1,0:T(8,128)(2,1)S(1)} %fusion.3), kind=kOutput, calls=%fused_computation.185 | convolution fusion | flops 402653184 | bytes 18882560 | tf_op jit(solution)/shard_map/ab,skbc->skac/dot_general | solution.py:30
  211.2 6.3 %fusion.87 = f32[3,64,256,64]{2,3,1,0:T(8,128)} fusion(bf16[64,64,1,1]{1,0,3,2:T(8,128)(2,1)S(1)} %copy-done.53, bf16[3,64,64,256]{3,2,1,0:T(8,128)(2,1)S(1)} %fusion.3), kind=kOutput, calls=%fused_computation.186 | convolution fusion | flops 402653184 | bytes 18882560 | tf_op jit(solution)/shard_map/ab,skbc->skac/dot_general | solution.py:31
  217.5 27.0 %fusion = f32[3,64,64,256]{3,1,2,0:T(8,128)} fusion(f32[3,64,256,64]{2,3,1,0:T(8,128)S(1)} %fusion.4, f32[3,64,256,64]{2,3,1,0:T(8,128)} %fusion.87, f32[3,64,256,64]{2,3,1,0:T(8,128)} %fusion.86), kind=kLoop, calls=%fused_computation.4 | loop fusion | flops 6291456 | bytes 50331648 | tf_op jit(solution)/shard_map/add | solution.py:32
  244.5 8.3 %multiply_subtract_fusion = (f32[3,64,32,256]{3,1,2,0:T(8,128)}, f32[3,64,32,256]{3,1,2,0:T(8,128)}) fusion(f32[3,64,64,256]{3,1,2,0:T(8,128)} %fusion, f32[64,32]{0,1:T(8,128)S(1)} %copy-done.44, f32[64,32]{0,1:T(8,128)S(1)} %copy-done.45), kind=kLoop, calls=%fused_computation.18 | loop fusion | flops 9437184 | bytes 25182208 | tf_op jit(solution)/shard_map/sub | solution.py:79
  252.8 8.3 %fusion.1 = bf16[3,128,32,256]{3,1,2,0:T(8,128)(2,1)} fusion(f32[3,64,32,256]{3,1,2,0:T(8,128)} %get-tuple-element.37, f32[3,64,32,256]{3,1,2,0:T(8,128)} %get-tuple-element.36), kind=kLoop, calls=%fused_computation.11 | loop fusion | flops 12582912 | bytes 18874368 | tf_op jit(solution)/shard_map/convert_element_type | solution.py:28
  261.1 7.5 %fusion.7 = f32[3,32,256,32]{2,3,1,0:T(8,128)S(1)} fusion(bf16[32,128,1,1]{1,0,3,2:T(8,128)(2,1)S(1)} %copy-done.49, bf16[3,128,32,256]{3,1,2,0:T(8,128)(2,1)} %fusion.1, f32[3,64,32,256]{3,1,2,0:T(8,128)} %get-tuple-element.37, f32[3,64,32,256]{3,1,2,0:T(8,128)} %get-tuple-element.36), kind=kOutput, calls=%fused_computation.21 | convolution fusion | flops 213909504 | bytes 22028288 | tf_op jit(solution)/shard_map/nk,skqb->snqb/dot_general | solution.py:32
  283.2 36.6 %all-to-all-done.1 = bf16[3,8,130,256]{3,2,0,1:T(8,128)(2,1)S(1)} async-done(((bf16[3,8,130,256]{3,2,0,1:T(8,128)(2,1)}), bf16[3,8,130,256]{3,2,0,1:T(8,128)(2,1)S(1)}, u32[]{:S(2)}, u32[]{:S(2)}) %all-to-all-start.1) | async-done | bytes 1597472 | tf_op jit(solution)/shard_map/all_to_all | solution.py:143
  341.1 118.1 %all-reduce.3.cloned.1.call-done = f32[10,2048]{1,0:T(8,128)} async-done(((f32[10,2048]{1,0:T(8,128)}), f32[10,2048]{1,0:T(8,128)}) %all-reduce.3.cloned.1.call-update) | async-done | bytes 81936 | tf_op jit(solution)/shard_map/psum | solution.py:174
  (200 shorter events, 74.8 us)
Async XLA Ops:
  8.0 27.4 %copy-start.22 = (bf16[1,128,2048]{2,1,0:T(8,128)(2,1)S(1)}, bf16[1,128,2048]{2,1,0:T(8,128)(2,1)}, u32[]{:S(2)}) copy-start(bf16[1,128,2048]{2,1,0:T(8,128)(2,1)} %param.22) | copy-start | bytes 1572868
  8.9 26.6 %collective-permute-start.4 = (bf16[2,2048]{1,0:T(2,128)(2,1)S(1)}, bf16[2,2048]{1,0:T(2,128)(2,1)S(1)}, u32[]{:S(2)}, u32[]{:S(2)}) collective-permute-start(bf16[2,2048]{1,0:T(2,128)(2,1)S(1)} %get-tuple-element.58), channel_id=1, source_target_pairs={{0,1},{1,2},{2,3},{3,4},{4,5},{5,6},{6,7},{8,9},{9,10},{10,11},{11... | collective-permute-start | bytes 24584 | tf_op jit(solution)/shard_map/ppermute | solution.py:13
  13.7 21.7 %collective-permute-start.5 = (bf16[2,2048]{1,0:T(2,128)(2,1)S(1)}, bf16[2,2048]{1,0:T(2,128)(2,1)S(1)}, u32[]{:S(2)}, u32[]{:S(2)}) collective-permute-start(bf16[2,2048]{1,0:T(2,128)(2,1)S(1)} %get-tuple-element.59), channel_id=1, source_target_pairs={{1,0},{2,1},{3,2},{4,3},{5,4},{6,5},{7,6},{9,8},{10,9},{11,10},{12... | collective-permute-start | bytes 24584 | tf_op jit(solution)/shard_map/ppermute | solution.py:13
  15.8 15.7 %collective-permute-start.2 = (bf16[2,2048]{1,0:T(2,128)(2,1)S(1)}, bf16[2,2048]{1,0:T(2,128)(2,1)S(1)}, u32[]{:S(2)}, u32[]{:S(2)}) collective-permute-start(bf16[2,2048]{1,0:T(2,128)(2,1)S(1)} %get-tuple-element.60), channel_id=1, source_target_pairs={{0,1},{1,2},{2,3},{3,4},{4,5},{5,6},{6,7},{8,9},{9,10},{10,11},{11... | collective-permute-start | bytes 24584 | tf_op jit(solution)/shard_map/ppermute | solution.py:13
  20.4 12.5 %collective-permute-start.3 = (bf16[2,2048]{1,0:T(2,128)(2,1)S(1)}, bf16[2,2048]{1,0:T(2,128)(2,1)S(1)}, u32[]{:S(2)}, u32[]{:S(2)}) collective-permute-start(bf16[2,2048]{1,0:T(2,128)(2,1)S(1)} %get-tuple-element.61), channel_id=1, source_target_pairs={{1,0},{2,1},{3,2},{4,3},{5,4},{6,5},{7,6},{9,8},{10,9},{11,10},{12... | collective-permute-start | bytes 24584 | tf_op jit(solution)/shard_map/ppermute | solution.py:13
  22.5 15.7 %collective-permute-start = (bf16[2,2048]{1,0:T(2,128)(2,1)S(1)}, bf16[2,2048]{1,0:T(2,128)(2,1)S(1)}, u32[]{:S(2)}, u32[]{:S(2)}) collective-permute-start(bf16[2,2048]{1,0:T(2,128)(2,1)S(1)} %get-tuple-element.62), channel_id=1, source_target_pairs={{0,1},{1,2},{2,3},{3,4},{4,5},{5,6},{6,7},{8,9},{9,10},{10,11},{11... | collective-permute-start | bytes 24584 | tf_op jit(solution)/shard_map/ppermute | solution.py:13
  30.8 7.3 %copy-start.25 = (f32[1,1,2048]{2,1,0:T(1,128)}, f32[1,1,2048]{2,1,0:T(1,128)S(1)}, u32[]{:S(2)}) copy-start(f32[1,1,2048]{2,1,0:T(1,128)S(1)} %get-tuple-element.65) | copy-start | bytes 24580
  30.8 7.3 %copy-start.27 = (f32[1,1,2048]{2,1,0:T(1,128)}, f32[1,1,2048]{2,1,0:T(1,128)S(1)}, u32[]{:S(2)}) copy-start(f32[1,1,2048]{2,1,0:T(1,128)S(1)} %get-tuple-element.66) | copy-start | bytes 24580
  30.8 7.3 %copy-start.29 = (f32[1,1,2048]{2,1,0:T(1,128)}, f32[1,1,2048]{2,1,0:T(1,128)S(1)}, u32[]{:S(2)}) copy-start(f32[1,1,2048]{2,1,0:T(1,128)S(1)} %get-tuple-element.67) | copy-start | bytes 24580
  30.8 7.3 %copy-start.31 = (f32[1,1,2048]{2,1,0:T(1,128)}, f32[1,1,2048]{2,1,0:T(1,128)S(1)}, u32[]{:S(2)}) copy-start(f32[1,1,2048]{2,1,0:T(1,128)S(1)} %get-tuple-element.64) | copy-start | bytes 24580
  30.8 7.3 %copy-start.33 = (f32[1,1,2048]{2,1,0:T(1,128)}, f32[1,1,2048]{2,1,0:T(1,128)S(1)}, u32[]{:S(2)}) copy-start(f32[1,1,2048]{2,1,0:T(1,128)S(1)} %get-tuple-element.71) | copy-start | bytes 24580
  30.9 9.1 %copy-start.37 = (f32[1,1,2048]{2,1,0:T(1,128)}, f32[1,1,2048]{2,1,0:T(1,128)S(1)}, u32[]{:S(2)}) copy-start(f32[1,1,2048]{2,1,0:T(1,128)S(1)} %get-tuple-element.68) | copy-start | bytes 24580
  30.9 9.1 %copy-start.39 = (f32[1,1,2048]{2,1,0:T(1,128)}, f32[1,1,2048]{2,1,0:T(1,128)S(1)}, u32[]{:S(2)}) copy-start(f32[1,1,2048]{2,1,0:T(1,128)S(1)} %get-tuple-element.69) | copy-start | bytes 24580
  30.9 9.1 %copy-start.41 = (f32[1,1,2048]{2,1,0:T(1,128)}, f32[1,1,2048]{2,1,0:T(1,128)S(1)}, u32[]{:S(2)}) copy-start(f32[1,1,2048]{2,1,0:T(1,128)S(1)} %get-tuple-element.70) | copy-start | bytes 24580
  31.6 6.6 %collective-permute-start.1 = (bf16[2,2048]{1,0:T(2,128)(2,1)S(1)}, bf16[2,2048]{1,0:T(2,128)(2,1)S(1)}, u32[]{:S(2)}, u32[]{:S(2)}) collective-permute-start(bf16[2,2048]{1,0:T(2,128)(2,1)S(1)} %get-tuple-element.63), channel_id=1, source_target_pairs={{1,0},{2,1},{3,2},{4,3},{5,4},{6,5},{7,6},{9,8},{10,9},{11,10},{12... | collective-permute-start | bytes 24584 | tf_op jit(solution)/shard_map/ppermute | solution.py:13
  32.9 7.1 %collective-permute-start.6 = (bf16[2,2048]{1,0:T(2,128)(2,1)S(1)}, bf16[2,2048]{1,0:T(2,128)(2,1)S(1)}, u32[]{:S(2)}, u32[]{:S(2)}) collective-permute-start(bf16[2,2048]{1,0:T(2,128)(2,1)S(1)} %slice_bitcast_fusion.13), channel_id=1, source_target_pairs={{1,0},{2,1},{3,2},{4,3},{5,4},{6,5},{7,6},{9,8},{10,9},{11,10},{12... | collective-permute-start | bytes 24584 | tf_op jit(solution)/shard_map/ppermute | solution.py:13
  120.8 8.5 %copy-start.1 = (bf16[3,64,64,256]{3,1,2,0:T(8,128)(2,1)S(1)}, bf16[3,64,64,256]{3,1,2,0:T(8,128)(2,1)}, u32[]{:S(2)}) copy-start(bf16[3,64,64,256]{3,1,2,0:T(8,128)(2,1)} %fusion.2) | copy-start | bytes 18874372
  120.8 8.5 %copy-start.46 = (bf16[64,64,1,1]{1,0,3,2:T(8,128)(2,1)S(1)}, bf16[64,64,1,1]{1,0,3,2:T(8,128)(2,1)}, u32[]{:S(2)}) copy-start(bf16[64,64,1,1]{1,0,3,2:T(8,128)(2,1)} %constant.62) | copy-start | bytes 24580
  138.8 9.5 %copy-start.50 = (bf16[64,64,1,1]{1,0,3,2:T(8,128)(2,1)S(1)}, bf16[64,64,1,1]{1,0,3,2:T(8,128)(2,1)}, u32[]{:S(2)}) copy-start(bf16[64,64,1,1]{1,0,3,2:T(8,128)(2,1)} %constant.63) | copy-start | bytes 24580
  252.8 8.3 %copy-start.49 = (bf16[32,128,1,1]{1,0,3,2:T(8,128)(2,1)S(1)}, bf16[32,128,1,1]{1,0,3,2:T(8,128)(2,1)}, u32[]{:S(2)}) copy-start(bf16[32,128,1,1]{1,0,3,2:T(8,128)(2,1)} %constant.66) | copy-start | bytes 24580
  261.1 8.3 %copy-start = (bf16[3,128,32,256]{3,1,2,0:T(8,128)(2,1)S(1)}, bf16[3,128,32,256]{3,1,2,0:T(8,128)(2,1)}, u32[]{:S(2)}) copy-start(bf16[3,128,32,256]{3,1,2,0:T(8,128)(2,1)} %fusion.1) | copy-start | bytes 18874372
  278.0 41.8 %all-to-all-start.1 = ((bf16[3,8,130,256]{3,2,0,1:T(8,128)(2,1)}), bf16[3,8,130,256]{3,2,0,1:T(8,128)(2,1)S(1)}, u32[]{:S(2)}, u32[]{:S(2)}) async-start(bf16[3,8,130,256]{3,2,0,1:T(8,128)(2,1)} %fusion.67), calls=%async_computation.1 | async-start | bytes 3342336 | tf_op jit(solution)/shard_map/all_to_all | solution.py:143
  281.7 177.6 %all-reduce.3.cloned.1.call-start = ((), (), s32[]{:S(2)}) async-start(), calls=%async_computation.4 | async-start | bytes 262144 | tf_op jit(solution)/shard_map/psum | solution.py:174
  337.8 124.5 %reduce-scatter.2.cloned.1.call-start = ((), (), s32[]{:S(2)}) async-start(), calls=%async_computation.3 | async-start | bytes 1310720 | tf_op jit(solution)/shard_map/reduce_scatter | solution.py:175
  (45 other events, 116.6 us)
Sparse Core Ops, SparseCore 0:
  337.9 121.2 all-reduce.2
Sparse Core Ops, SparseCore 1:
  340.8 23.7 reduce-scatter.1
where the time goes:
time: 480 us; the launch traced here: 472 us
  waiting for transfers between devices  156 us (32%)
  other arithmetic  115 us (24%)
  matrix products  65.5 us (14%)
  blocking collectives  54.8 us (11%)
  local copies, waits for them, and re-layouts  40.2 us (8%)
  starting transfers between devices  23.3 us (5%)
  between operations  16.6 us (3%)
    psum x1, waiting for transfers between devices, local(): summed = lax.psum(stats, ('dp', 'ctx'))  118 us
    all_to_all x1, blocking collectives, local(): columns = lax.all_to_all(sent, 'ctx', 2, 1, tiled=True)  54.8 us
    all_to_all x1, waiting for transfers between devices, local(): lax.all_to_all(blocks, 'ctx', 1, 3, tiled=True).reshape(3, ext, chans)  36.6 us
    add x1, other arithmetic, split_product(): total + jnp.einsum(form, upper, data_lower, preferred_element_type=wide)  27 us
    dot_general x3, matrix products, split_product(): jnp.einsum(form, upper, data_lower, preferred_element_type=wide)  22.9 us
    dot_general x3, matrix products, split_product(): jnp.einsum(form, lower, data_upper, preferred_element_type=wide)  21.8 us
    convert_element_type x3, other arithmetic, split_product(): data_upper = lax.optimization_barrier(data.astype(jnp.bfloat16))  21.6 us
    ppermute x7, starting transfers between devices, shifted(): return lax.ppermute(x, axis, pairs)  19.5 us
  transfers between devices with their start and end apart: 10, of which 3 were waited for; matrix products, arithmetic and copies ran while one was open for 4% of the time, Pallas kernels for 0%

commit v1 on v0

--- a/solution.py
+++ b/solution.py
@@ -171,7 +171,7 @@
     stats = jnp.concatenate(
         [jnp.stack([short_q, short_k, short_v]).reshape(3 * taps, chans), skip_grad[None]], 0
     )
-    summed = lax.psum(stats, ("dp", "ctx"))
+    summed = lax.psum(lax.psum(stats, "ctx"), "dp")
     filter_part = lax.psum_scatter(back[2, :rows], "dp", scatter_dimension=1, tiled=True)
     scale = 1.0 / (groups * seq_len)
     return (

time: 480 us -> 480 us (level)
    psum x1 -> x2, waiting for transfers between devices: 118 us -> 92.6 us  [local(): summed = lax.psum(lax.psum(stats, 'ctx'), 'dp')]
    reduce_scatter x1, waiting for transfers between devices: 0.01 us -> 24.4 us  [local(): lax.psum_scatter(back[2, :rows], 'dp', scatter_dimension=1, tiled=True)]
    unnamed x129 -> x127, local copies, waits for them, and re-layouts: 10.8 us -> 9.1 us
  transfers between devices with their start and end apart: 10 -> 11, of which waited for: 3 -> 5; matrix products, arithmetic and copies ran while one was open for 4% -> 5% of each run, Pallas kernels for 0% -> 0%
where the time goes in v1:
time: 480 us; the launch traced here: 471 us
  waiting for transfers between devices  156 us (32%)
  other arithmetic  118 us (25%)
  matrix products  65.5 us (14%)
  blocking collectives  54.9 us (11%)
  local copies, waits for them, and re-layouts  38 us (8%)
  starting transfers between devices  24.1 us (5%)
  between operations  14.8 us (3%)
    psum x2, waiting for transfers between devices, local(): summed = lax.psum(lax.psum(stats, 'ctx'), 'dp')  92.6 us
    all_to_all x1, blocking collectives, local(): columns = lax.all_to_all(sent, 'ctx', 2, 1, tiled=True)  54.9 us
    all_to_all x1, waiting for transfers between devices, local(): lax.all_to_all(blocks, 'ctx', 1, 3, tiled=True).reshape(3, ext, chans)  37.3 us
    add x1, other arithmetic, split_product(): total + jnp.einsum(form, upper, data_lower, preferred_element_type=wide)  27 us
    reduce_scatter x1, waiting for transfers between devices, local(): lax.psum_scatter(back[2, :rows], 'dp', scatter_dimension=1, tiled=True)  24.4 us
    dot_general x3, matrix products, split_product(): jnp.einsum(form, upper, data_lower, preferred_element_type=wide)  22.9 us
    dot_general x3, matrix products, split_product(): jnp.einsum(form, lower, data_upper, preferred_element_type=wide)  21.8 us
    convert_element_type x3, other arithmetic, split_product(): data_upper = lax.optimization_barrier(data.astype(jnp.bfloat16))  21.5 us
  transfers between devices with their start and end apart: 11, of which 5 were waited for; matrix products, arithmetic and copies ran while one was open for 5% of the time, Pallas kernels for 0%

profile of v1, /device:TPU:0, one launch (start us, length us, event | category | flops | bytes accessed | tf_op | source)
XLA Modules:
  0.0 471.3 jit_solution(3163852032216435331)
XLA Ops:
  8.0 4.9 %collective-permute-start.4 = (bf16[2,2048]{1,0:T(2,128)(2,1)S(1)}, bf16[2,2048]{1,0:T(2,128)(2,1)S(1)}, u32[]{:S(2)}, u32[]{:S(2)}) collective-permute-start(bf16[2,2048]{1,0:T(2,128)(2,1)S(1)} %get-tuple-element.58), channel_id=1, source_target_pairs={{0,1},{1,2},{2,3},{3,4},{4,5},{5,6},{6,7},{8,9},{9,10},{10,11},{11... | collective-permute-start | bytes 24584 | tf_op jit(solution)/shard_map/ppermute | solution.py:13
  21.7 5.0 %collective-permute-start = (bf16[2,2048]{1,0:T(2,128)(2,1)S(1)}, bf16[2,2048]{1,0:T(2,128)(2,1)S(1)}, u32[]{:S(2)}, u32[]{:S(2)}) collective-permute-start(bf16[2,2048]{1,0:T(2,128)(2,1)S(1)} %get-tuple-element.62), channel_id=1, source_target_pairs={{0,1},{1,2},{2,3},{3,4},{4,5},{5,6},{6,7},{8,9},{9,10},{10,11},{11... | collective-permute-start | bytes 24584 | tf_op jit(solution)/shard_map/ppermute | solution.py:13
  46.8 54.9 %all_to_all.24 = bf16[3,128,2048]{1,0,2:T(4,128)(2,1)S(1)} all-to-all(bf16[3,128,2048]{1,0,2:T(4,128)(2,1)S(1)} %copy.95), channel_id=1, replica_groups=mesh['dp'=4,'ctx'=8] {'ctx'}, dimensions={2} | all-to-all | bytes 3145728 | tf_op jit(solution)/shard_map/all_to_all | solution.py:138
  106.7 5.4 %multiply_add_fusion.1 = (f32[3,64,32,256]{3,1,2,0:T(8,128)}, f32[3,64,32,256]{3,1,2,0:T(8,128)}) fusion(f32[3,128,32,256]{3,1,2,0:T(8,128)S(1)} %add_bitcast_fusion.1, f32[64,32]{0,1:T(8,128)S(1)} %copy-done.43, f32[64,32]{0,1:T(8,128)S(1)} %copy-done.44), kind=kLoop, calls=%fused_computation.20 | loop fusion | flops 9437184 | bytes 25182208 | tf_op jit(solution)/shard_map/add | solution.py:65
  112.1 7.9 %fusion.2 = bf16[3,64,64,256]{3,1,2,0:T(8,128)(2,1)} fusion(f32[3,64,32,256]{3,1,2,0:T(8,128)} %get-tuple-element.39, f32[3,64,32,256]{3,1,2,0:T(8,128)} %get-tuple-element.38), kind=kLoop, calls=%fused_computation.12 | loop fusion | flops 3145728 | bytes 18874368 | tf_op jit(solution)/shard_map/convert_element_type | solution.py:28
  120.0 8.5 %subtract_convert_fusion.2 = bf16[3,64,64,256]{3,1,2,0:T(8,128)(2,1)S(1)} fusion(bf16[3,64,64,256]{3,1,2,0:T(8,128)(2,1)} %fusion.2, f32[3,64,32,256]{3,1,2,0:T(8,128)} %get-tuple-element.39, f32[3,64,32,256]{3,1,2,0:T(8,128)} %get-tuple-element.38), kind=kLoop, calls=%fused_computation.9 | loop fusion | flops 12582912 | bytes 25165824 | tf_op jit(solution)/shard_map/convert_element_type | solution.py:29
  128.5 9.5 %fusion.8 = f32[3,64,256,64]{2,3,1,0:T(8,128)} fusion(bf16[64,64,1,1]{1,0,3,2:T(8,128)(2,1)S(1)} %copy-done.45, bf16[3,64,64,256]{3,1,2,0:T(8,128)(2,1)S(1)} %copy-done.1), kind=kOutput, calls=%fused_computation.22 | convolution fusion | flops 402653184 | bytes 18882560 | tf_op jit(solution)/shard_map/ab,skbc->skac/dot_general | solution.py:30
  138.0 9.5 %fusion.5 = f32[3,64,256,64]{2,3,1,0:T(8,128)} fusion(bf16[64,64,1,1]{1,0,3,2:T(8,128)(2,1)S(1)} %copy-done.45, bf16[3,64,64,256]{3,1,2,0:T(8,128)(2,1)S(1)} %subtract_convert_fusion.2), kind=kOutput, calls=%fused_computation.15 | convolution fusion | flops 402653184 | bytes 18882560 | tf_op jit(solution)/shard_map/ab,skbc->skac/dot_general | solution.py:32
  147.5 14.4 %add_bitcast_fusion = f32[3,64,64,256]{3,2,1,0:T(8,128)} fusion(f32[3,64,256,64]{2,3,1,0:T(8,128)} %fusion.5, f32[3,64,256,64]{2,3,1,0:T(8,128)} %fusion.8, bf16[64,64,1,1]{1,0,3,2:T(8,128)(2,1)S(1)} %copy-done.49, bf16[3,64,64,256]{3,1,2,0:T(8,128)(2,1)S(1)} %copy-done.1), kind=kOutput, calls=%fused_computation.8 | convolution fusion | flops 408944640 | bytes 44048384 | tf_op jit(solution)/shard_map/ab,skbc->skac/dot_general | solution.py:31
  161.9 10.0 %slice_bitcast_fusion.1 = (f32[64,64,256]{2,1,0:T(8,128)S(1)}, f32[64,64,256]{2,1,0:T(8,128)}, f32[64,64,256]{2,1,0:T(8,128)}) fusion(f32[3,64,64,256]{3,2,1,0:T(8,128)} %add_bitcast_fusion), kind=kLoop, calls=%fused_computation.27 | loop fusion | bytes 25165824 | tf_op jit(solution)/shard_map/squeeze | solution.py:88
  171.9 5.4 %multiply_add_fusion.3 = (f32[64,32,256]{2,1,0:T(8,128)}, f32[64,32,256]{2,1,0:T(8,128)}) fusion(f32[64,64,256]{2,1,0:T(8,128)} %get-tuple-element.41, f32[64,64,256]{2,1,0:T(8,128)S(1)} %get-tuple-element.40), kind=kLoop, calls=%fused_computation.37 | loop fusion | flops 3145728 | bytes 12582912 | tf_op jit(solution)/shard_map/add | solution.py:91
  177.3 5.8 %multiply_subtract_fusion.4 = (f32[64,32,256]{2,1,0:T(8,128)}, f32[64,32,256]{2,1,0:T(8,128)}, f32[64,32,256]{2,1,0:T(8,128)S(1)}, f32[64,32,256]{2,1,0:T(8,128)S(1)}) fusion(f32[64,64,256]{2,1,0:T(8,128)S(1)} %get-tuple-element.40, f32[64,64,256]{2,1,0:T(8,128)} %get-tuple-element.42, f32[64,64,256]{2,1,0:T(8,128)S(1)} %copy-done.8), kind=kLoop, calls=%fused_computation.39 | loop fusion | flops 6291456 | bytes 20971520 | tf_op jit(solution)/shard_map/sub | solution.py:90
  192.8 5.4 %fusion.3 = bf16[3,64,64,256]{3,2,1,0:T(8,128)(2,1)S(1)} fusion(f32[1,64,64,256]{3,2,1,0:T(8,128)} %maximum_bitcast_fusion.2, f32[1,64,64,256]{3,2,1,0:T(8,128)} %maximum_bitcast_fusion.1, f32[1,64,64,256]{3,2,1,0:T(8,128)} %maximum_bitcast_fusion), kind=kLoop, calls=%fused_computation.13 | loop fusion | flops 6291456 | bytes 18874368 | tf_op jit(solution)/shard_map/convert_element_type | solution.py:28
  198.2 5.9 %fusion.4 = f32[3,64,256,64]{2,3,1,0:T(8,128)S(1)} fusion(bf16[64,64,1,1]{1,0,3,2:T(8,128)(2,1)S(1)} %copy-done.42, bf16[3,64,64,256]{3,2,1,0:T(8,128)(2,1)S(1)} %fusion.3, f32[1,64,64,256]{3,2,1,0:T(8,128)} %maximum_bitcast_fusion.2, f32[1,64,64,256]{3,2,1,0:T(8,128)} %maximum_bitcast_fusion.1, f32[1,64,64,256]{3,2,1,0:T(8,128)} %maximum_bitcast_fusion), kind=kOutput, calls=%fused_computation.14 | convolution fusion | flops 418381824 | bytes 31465472 | tf_op jit(solution)/shard_map/ab,skbc->skac/dot_general | solution.py:32
  204.0 6.4 %fusion.86 = f32[3,64,256,64]{2,3,1,0:T(8,128)} fusion(bf16[64,64,1,1]{1,0,3,2:T(8,128)(2,1)S(1)} %copy-done.42, bf16[3,64,64,256]{3,2,1,0:T(8,128)(2,1)S(1)} %fusion.3), kind=kOutput, calls=%fused_computation.185 | convolution fusion | flops 402653184 | bytes 18882560 | tf_op jit(solution)/shard_map/ab,skbc->skac/dot_general | solution.py:30
  210.4 6.3 %fusion.87 = f32[3,64,256,64]{2,3,1,0:T(8,128)} fusion(bf16[64,64,1,1]{1,0,3,2:T(8,128)(2,1)S(1)} %copy-done.52, bf16[3,64,64,256]{3,2,1,0:T(8,128)(2,1)S(1)} %fusion.3), kind=kOutput, calls=%fused_computation.186 | convolution fusion | flops 402653184 | bytes 18882560 | tf_op jit(solution)/shard_map/ab,skbc->skac/dot_general | solution.py:31
  216.7 27.0 %fusion = f32[3,64,64,256]{3,1,2,0:T(8,128)} fusion(f32[3,64,256,64]{2,3,1,0:T(8,128)S(1)} %fusion.4, f32[3,64,256,64]{2,3,1,0:T(8,128)} %fusion.87, f32[3,64,256,64]{2,3,1,0:T(8,128)} %fusion.86), kind=kLoop, calls=%fused_computation.4 | loop fusion | flops 6291456 | bytes 50331648 | tf_op jit(solution)/shard_map/add | solution.py:32
  243.7 8.3 %multiply_subtract_fusion = (f32[3,64,32,256]{3,1,2,0:T(8,128)}, f32[3,64,32,256]{3,1,2,0:T(8,128)}) fusion(f32[3,64,64,256]{3,1,2,0:T(8,128)} %fusion, f32[64,32]{0,1:T(8,128)S(1)} %copy-done.43, f32[64,32]{0,1:T(8,128)S(1)} %copy-done.44), kind=kLoop, calls=%fused_computation.18 | loop fusion | flops 9437184 | bytes 25182208 | tf_op jit(solution)/shard_map/sub | solution.py:79
  252.0 8.2 %fusion.1 = bf16[3,128,32,256]{3,1,2,0:T(8,128)(2,1)} fusion(f32[3,64,32,256]{3,1,2,0:T(8,128)} %get-tuple-element.37, f32[3,64,32,256]{3,1,2,0:T(8,128)} %get-tuple-element.36), kind=kLoop, calls=%fused_computation.11 | loop fusion | flops 12582912 | bytes 18874368 | tf_op jit(solution)/shard_map/convert_element_type | solution.py:28
  260.2 7.5 %fusion.7 = f32[3,32,256,32]{2,3,1,0:T(8,128)S(1)} fusion(bf16[32,128,1,1]{1,0,3,2:T(8,128)(2,1)S(1)} %copy-done.48, bf16[3,128,32,256]{3,1,2,0:T(8,128)(2,1)} %fusion.1, f32[3,64,32,256]{3,1,2,0:T(8,128)} %get-tuple-element.37, f32[3,64,32,256]{3,1,2,0:T(8,128)} %get-tuple-element.36), kind=kOutput, calls=%fused_computation.21 | convolution fusion | flops 213909504 | bytes 22028288 | tf_op jit(solution)/shard_map/nk,skqb->snqb/dot_general | solution.py:32
  281.8 37.3 %all-to-all-done.1 = bf16[3,8,130,256]{3,2,0,1:T(8,128)(2,1)} async-done(((bf16[3,8,130,256]{3,2,0,1:T(8,128)(2,1)}), bf16[3,8,130,256]{3,2,0,1:T(8,128)(2,1)}, u32[]{:S(2)}, u32[]{:S(2)}) %all-to-all-start.1) | async-done | bytes 1597472 | tf_op jit(solution)/shard_map/all_to_all | solution.py:143
  339.3 63.1 %all-reduce.4.cloned.1.call-done = f32[10,2048]{1,0:T(8,128)} async-done(((f32[10,2048]{1,0:T(8,128)}), f32[10,2048]{1,0:T(8,128)}) %all-reduce.4.cloned.1.call-update) | async-done | bytes 81936 | tf_op jit(solution)/shard_map/psum | solution.py:174
  406.0 29.5 %all-reduce.6.cloned.1.call-done = f32[10,2048]{1,0:T(8,128)} async-done(((f32[10,2048]{1,0:T(8,128)}), f32[10,2048]{1,0:T(8,128)}) %all-reduce.6.cloned.1.call-update) | async-done | bytes 81936 | tf_op jit(solution)/shard_map/psum | solution.py:174
  438.5 24.4 %reduce-scatter.2.cloned.1.call-done = f32[128,512]{1,0:T(8,128)} async-done(((f32[128,2048]{1,0:T(8,128)}), f32[128,512]{1,0:T(8,128)}) %reduce-scatter.2.cloned.1.call-update) | async-done | bytes 262160 | tf_op jit(solution)/shard_map/reduce_scatter | solution.py:175
  (201 shorter events, 86.1 us)
Async XLA Ops:
  7.2 27.5 %copy-start.21 = (bf16[1,128,2048]{2,1,0:T(8,128)(2,1)S(1)}, bf16[1,128,2048]{2,1,0:T(8,128)(2,1)}, u32[]{:S(2)}) copy-start(bf16[1,128,2048]{2,1,0:T(8,128)(2,1)} %param.22) | copy-start | bytes 1572868
  8.0 26.6 %collective-permute-start.4 = (bf16[2,2048]{1,0:T(2,128)(2,1)S(1)}, bf16[2,2048]{1,0:T(2,128)(2,1)S(1)}, u32[]{:S(2)}, u32[]{:S(2)}) collective-permute-start(bf16[2,2048]{1,0:T(2,128)(2,1)S(1)} %get-tuple-element.58), channel_id=1, source_target_pairs={{0,1},{1,2},{2,3},{3,4},{4,5},{5,6},{6,7},{8,9},{9,10},{10,11},{11... | collective-permute-start | bytes 24584 | tf_op jit(solution)/shard_map/ppermute | solution.py:13
  12.9 21.7 %collective-permute-start.5 = (bf16[2,2048]{1,0:T(2,128)(2,1)S(1)}, bf16[2,2048]{1,0:T(2,128)(2,1)S(1)}, u32[]{:S(2)}, u32[]{:S(2)}) collective-permute-start(bf16[2,2048]{1,0:T(2,128)(2,1)S(1)} %get-tuple-element.59), channel_id=1, source_target_pairs={{1,0},{2,1},{3,2},{4,3},{5,4},{6,5},{7,6},{9,8},{10,9},{11,10},{12... | collective-permute-start | bytes 24584 | tf_op jit(solution)/shard_map/ppermute | solution.py:13
  15.0 15.8 %collective-permute-start.2 = (bf16[2,2048]{1,0:T(2,128)(2,1)S(1)}, bf16[2,2048]{1,0:T(2,128)(2,1)S(1)}, u32[]{:S(2)}, u32[]{:S(2)}) collective-permute-start(bf16[2,2048]{1,0:T(2,128)(2,1)S(1)} %get-tuple-element.60), channel_id=1, source_target_pairs={{0,1},{1,2},{2,3},{3,4},{4,5},{5,6},{6,7},{8,9},{9,10},{10,11},{11... | collective-permute-start | bytes 24584 | tf_op jit(solution)/shard_map/ppermute | solution.py:13
  19.6 12.5 %collective-permute-start.3 = (bf16[2,2048]{1,0:T(2,128)(2,1)S(1)}, bf16[2,2048]{1,0:T(2,128)(2,1)S(1)}, u32[]{:S(2)}, u32[]{:S(2)}) collective-permute-start(bf16[2,2048]{1,0:T(2,128)(2,1)S(1)} %get-tuple-element.61), channel_id=1, source_target_pairs={{1,0},{2,1},{3,2},{4,3},{5,4},{6,5},{7,6},{9,8},{10,9},{11,10},{12... | collective-permute-start | bytes 24584 | tf_op jit(solution)/shard_map/ppermute | solution.py:13
  21.7 15.7 %collective-permute-start = (bf16[2,2048]{1,0:T(2,128)(2,1)S(1)}, bf16[2,2048]{1,0:T(2,128)(2,1)S(1)}, u32[]{:S(2)}, u32[]{:S(2)}) collective-permute-start(bf16[2,2048]{1,0:T(2,128)(2,1)S(1)} %get-tuple-element.62), channel_id=1, source_target_pairs={{0,1},{1,2},{2,3},{3,4},{4,5},{5,6},{6,7},{8,9},{9,10},{10,11},{11... | collective-permute-start | bytes 24584 | tf_op jit(solution)/shard_map/ppermute | solution.py:13
  30.0 7.3 %copy-start.24 = (f32[1,1,2048]{2,1,0:T(1,128)}, f32[1,1,2048]{2,1,0:T(1,128)S(1)}, u32[]{:S(2)}) copy-start(f32[1,1,2048]{2,1,0:T(1,128)S(1)} %get-tuple-element.65) | copy-start | bytes 24580
  30.0 7.3 %copy-start.26 = (f32[1,1,2048]{2,1,0:T(1,128)}, f32[1,1,2048]{2,1,0:T(1,128)S(1)}, u32[]{:S(2)}) copy-start(f32[1,1,2048]{2,1,0:T(1,128)S(1)} %get-tuple-element.66) | copy-start | bytes 24580
  30.0 7.3 %copy-start.28 = (f32[1,1,2048]{2,1,0:T(1,128)}, f32[1,1,2048]{2,1,0:T(1,128)S(1)}, u32[]{:S(2)}) copy-start(f32[1,1,2048]{2,1,0:T(1,128)S(1)} %get-tuple-element.67) | copy-start | bytes 24580
  30.0 7.3 %copy-start.30 = (f32[1,1,2048]{2,1,0:T(1,128)}, f32[1,1,2048]{2,1,0:T(1,128)S(1)}, u32[]{:S(2)}) copy-start(f32[1,1,2048]{2,1,0:T(1,128)S(1)} %get-tuple-element.64) | copy-start | bytes 24580
  30.0 9.1 %copy-start.36 = (f32[1,1,2048]{2,1,0:T(1,128)}, f32[1,1,2048]{2,1,0:T(1,128)S(1)}, u32[]{:S(2)}) copy-start(f32[1,1,2048]{2,1,0:T(1,128)S(1)} %get-tuple-element.68) | copy-start | bytes 24580
  30.0 9.1 %copy-start.38 = (f32[1,1,2048]{2,1,0:T(1,128)}, f32[1,1,2048]{2,1,0:T(1,128)S(1)}, u32[]{:S(2)}) copy-start(f32[1,1,2048]{2,1,0:T(1,128)S(1)} %get-tuple-element.69) | copy-start | bytes 24580
  30.1 9.1 %copy-start.40 = (f32[1,1,2048]{2,1,0:T(1,128)}, f32[1,1,2048]{2,1,0:T(1,128)S(1)}, u32[]{:S(2)}) copy-start(f32[1,1,2048]{2,1,0:T(1,128)S(1)} %get-tuple-element.70) | copy-start | bytes 24580
  30.8 6.6 %collective-permute-start.1 = (bf16[2,2048]{1,0:T(2,128)(2,1)S(1)}, bf16[2,2048]{1,0:T(2,128)(2,1)S(1)}, u32[]{:S(2)}, u32[]{:S(2)}) collective-permute-start(bf16[2,2048]{1,0:T(2,128)(2,1)S(1)} %get-tuple-element.63), channel_id=1, source_target_pairs={{1,0},{2,1},{3,2},{4,3},{5,4},{6,5},{7,6},{9,8},{10,9},{11,10},{12... | collective-permute-start | bytes 24584 | tf_op jit(solution)/shard_map/ppermute | solution.py:13
  32.1 7.1 %collective-permute-start.6 = (bf16[2,2048]{1,0:T(2,128)(2,1)S(1)}, bf16[2,2048]{1,0:T(2,128)(2,1)S(1)}, u32[]{:S(2)}, u32[]{:S(2)}) collective-permute-start(bf16[2,2048]{1,0:T(2,128)(2,1)S(1)} %slice_bitcast_fusion.13), channel_id=1, source_target_pairs={{1,0},{2,1},{3,2},{4,3},{5,4},{6,5},{7,6},{9,8},{10,9},{11,10},{12... | collective-permute-start | bytes 24584 | tf_op jit(solution)/shard_map/ppermute | solution.py:13
  120.0 8.5 %copy-start.1 = (bf16[3,64,64,256]{3,1,2,0:T(8,128)(2,1)S(1)}, bf16[3,64,64,256]{3,1,2,0:T(8,128)(2,1)}, u32[]{:S(2)}) copy-start(bf16[3,64,64,256]{3,1,2,0:T(8,128)(2,1)} %fusion.2) | copy-start | bytes 18874372
  120.0 8.5 %copy-start.45 = (bf16[64,64,1,1]{1,0,3,2:T(8,128)(2,1)S(1)}, bf16[64,64,1,1]{1,0,3,2:T(8,128)(2,1)}, u32[]{:S(2)}) copy-start(bf16[64,64,1,1]{1,0,3,2:T(8,128)(2,1)} %constant.62) | copy-start | bytes 24580
  138.0 9.5 %copy-start.49 = (bf16[64,64,1,1]{1,0,3,2:T(8,128)(2,1)S(1)}, bf16[64,64,1,1]{1,0,3,2:T(8,128)(2,1)}, u32[]{:S(2)}) copy-start(bf16[64,64,1,1]{1,0,3,2:T(8,128)(2,1)} %constant.63) | copy-start | bytes 24580
  252.0 8.2 %copy-start.48 = (bf16[32,128,1,1]{1,0,3,2:T(8,128)(2,1)S(1)}, bf16[32,128,1,1]{1,0,3,2:T(8,128)(2,1)}, u32[]{:S(2)}) copy-start(bf16[32,128,1,1]{1,0,3,2:T(8,128)(2,1)} %constant.66) | copy-start | bytes 24580
  260.2 8.3 %copy-start = (bf16[3,128,32,256]{3,1,2,0:T(8,128)(2,1)S(1)}, bf16[3,128,32,256]{3,1,2,0:T(8,128)(2,1)}, u32[]{:S(2)}) copy-start(bf16[3,128,32,256]{3,1,2,0:T(8,128)(2,1)} %fusion.1) | copy-start | bytes 18874372
  277.1 42.0 %all-to-all-start.1 = ((bf16[3,8,130,256]{3,2,0,1:T(8,128)(2,1)}), bf16[3,8,130,256]{3,2,0,1:T(8,128)(2,1)}, u32[]{:S(2)}, u32[]{:S(2)}) async-start(bf16[3,8,130,256]{3,2,0,1:T(8,128)(2,1)} %fusion.67), calls=%async_computation.1 | async-start | bytes 3342336 | tf_op jit(solution)/shard_map/all_to_all | solution.py:143
  281.5 120.8 %all-reduce.4.cloned.1.call-start = ((), (), s32[]{:S(2)}) async-start(), calls=%async_computation.4 | async-start | bytes 262144 | tf_op jit(solution)/shard_map/psum | solution.py:174
  333.7 101.7 %all-reduce.6.cloned.1.call-start = ((), (), s32[]{:S(2)}) async-start(), calls=%async_computation.5 | async-start | bytes 262144 | tf_op jit(solution)/shard_map/psum | solution.py:174
  402.4 60.5 %reduce-scatter.2.cloned.1.call-start = ((), (), s32[]{:S(2)}) async-start(), calls=%async_computation.3 | async-start | bytes 1310720 | tf_op jit(solution)/shard_map/reduce_scatter | solution.py:175
  (45 other events, 126.4 us)
Sparse Core Ops, SparseCore 0:
  333.9 68.4 all-reduce.3
  404.8 30.6 all-reduce.5
  438.0 24.8 reduce-scatter.1
